TPU v7x, 32 devices: a whole 2x2x4 slice. The times are simulated.
32 devices in a mesh: groups: 2 (over y), row: 4 (over z), col: 2 (over x), mode: 2 (over core).
Axes of the slice: x: 2, y: 2, z: 4, core: 2. Of those that a mesh axis runs over, the one named last changes fastest.
Arguments:
- object_field: float32 [2, 1024, 256], P(None, ('groups', 'row'), 'col'), parts along dimension 1, may hold values from -6 to 6
- probe_modes: float32 [2, 2, 256, 256], P('mode'), may hold values from -1.5 to 1.5
- measured: bfloat16 [8, 2, 2, 256, 256], P(('groups', 'row'), 'col'), parts along dimension 0, may hold values from 0.049804688 to 2
- offset_rows: int32 [8, 2, 2], P(('groups', 'row'), 'col'), parts along dimension 0, may hold values from -128 to -1
- offset_cols: int32 [8, 2, 2], P(('groups', 'row'), 'col'), parts along dimension 0, may hold values from -128 to -1
- pattern_counts: int32 [8, 2], P(('groups', 'row'), 'col'), parts along dimension 0, may hold values from 0 to 2, as said below
Outputs:
- object_out: float32 [2, 1024, 256], P(None, ('groups', 'row'), 'col'), parts along dimension 1
There are 2 independent parts, one for each index of `groups`. A program takes and returns all parts, laid end to end along the dimension named above; an argument that names none is the same for every part. Nothing has to cross between parts.
Inputs may be any that keep to these rules, and one draw needn't show every extreme that they name: `pattern_counts`: slots at or beyond a tile's count are unused; some tile owns exactly 2 patterns.
All inputs are finite; a program needn't handle non-finite values.
Results may differ from a plain program's by a relative error of at most 0.0003.
Values sent between devices are 32-bit elements; how exact they have to be, the bound alone decides.
A program may use at most 64 MiB of HBM per device.

v0:
```python
import functools

import jax
import jax.numpy as jnp
import numpy as np
from jax import lax
from jax.experimental import pallas as pl
from jax.experimental.pallas import tpu as pltpu
from jax.sharding import PartitionSpec as P

ITERS = 2
STEP = 2.0
MESH = pl.DeviceIdType.MESH
DIRECTIONS = [(i, j) for i in (-1, 0, 1) for j in (-1, 0, 1) if (i, j) != (0, 0)]


def dft_tables(side):
    index = np.arange(side)
    angles = (index[:, None] * index[None, :] % side) * (2.0 * np.pi / side)
    tables = []
    for table in (np.cos(angles), np.sin(angles)):
        table = (table / np.sqrt(side)).astype(np.float32)
        high = table.astype(jnp.bfloat16)
        low = (table - high.astype(np.float32)).astype(jnp.bfloat16)
        tables += [high, low]
    return np.stack(tables)


def split(x):
    high = x.astype(jnp.bfloat16)
    return high, (x - high.astype(jnp.float32)).astype(jnp.bfloat16)


def dot(a, b):
    return jnp.dot(a, b, preferred_element_type=jnp.float32)


def dot3(a, b):
    return dot(a[0], b[0]) + (dot(a[0], b[1]) + dot(a[1], b[0]))


def kernel(rows_ref, cols_ref, counts_ref, field_ref, probe_ref, measured_ref, table_ref, out_ref,
           ext, grad, partner_grad, received, probe_other, lefts, rights,
           halo_send, halo_recv, fwd_send, fwd_recv, fold_send, fold_recv, own_send, own_recv):
    side = probe_ref.shape[-1]
    half = field_ref.shape[-1]
    n_row, n_col = lax.axis_size("row"), lax.axis_size("col")
    r, c, m = lax.axis_index("row"), lax.axis_index("col"), lax.axis_index("mode")
    other = 1 - m
    partner = {"mode": other}

    def exists(dr, dc):
        return (r + dr >= 0) & (r + dr < n_row) & (c + dc >= 0) & (c + dc < n_col)

    def block(ref, plane, i, j):
        return ref.at[plane, pl.ds(half * (1 + i), half), pl.ds(half * (1 + j), half)]

    for k, (dr, dc) in enumerate(DIRECTIONS):
        @pl.when(jnp.logical_not(exists(-dr, -dc)))
        def _():
            zeros = jnp.zeros((half, half), jnp.float32)
            received[k] = zeros
            for plane in range(2):
                ext[plane, half * (1 - dr):half * (2 - dr), half * (1 - dc):half * (2 - dc)] = zeros
    ext[0, half:2 * half, half:2 * half] = field_ref[0]
    ext[1, half:2 * half, half:2 * half] = field_ref[1]

    barrier = pltpu.get_barrier_semaphore()
    pl.semaphore_signal(barrier, inc=1, device_id=partner, device_id_type=MESH)
    count = 1
    for dr, dc in DIRECTIONS:
        here = exists(dr, dc)
        count = count + here.astype(jnp.int32)

        @pl.when(here)
        def _():
            pl.semaphore_signal(barrier, inc=1, device_id={"row": r + dr, "col": c + dc}, device_id_type=MESH)
    pl.semaphore_wait(barrier, count)

    def remote(src, dst, send, recv, device):
        return pltpu.make_async_remote_copy(
            src_ref=src, dst_ref=dst, send_sem=send, recv_sem=recv, device_id=device, device_id_type=MESH)

    def halo_copy(k):
        dr, dc = DIRECTIONS[k]
        return remote(block(ext, m, 0, 0), block(ext, m, -dr, -dc), halo_send.at[k], halo_recv.at[k],
                      {"row": r + dr, "col": c + dc})

    def forward_copy(k):
        dr, dc = DIRECTIONS[k]
        return remote(block(ext, m, -dr, -dc), block(ext, m, -dr, -dc), fwd_send.at[k], fwd_recv.at[k], partner)

    def fold_copy(k):
        dr, dc = DIRECTIONS[k]
        return remote(block(grad, m, dr, dc), received.at[k], fold_send.at[k], fold_recv.at[k],
                      {"row": r + dr, "col": c + dc})

    probe_copy = remote(probe_ref.at[0], probe_other, own_send.at[0], own_recv.at[0], partner)
    grad_copy = remote(grad.at[other], partner_grad, own_send.at[1], own_recv.at[1], partner)
    center_copy = remote(block(ext, m, 0, 0), block(ext, m, 0, 0), own_send.at[2], own_recv.at[2], partner)

    def start_halo():
        for k, (dr, dc) in enumerate(DIRECTIONS):
            @pl.when(exists(dr, dc))
            def _():
                halo_copy(k).start()

    def finish_halo():
        for k, (dr, dc) in enumerate(DIRECTIONS):
            @pl.when(exists(-dr, -dc))
            def _():
                halo_copy(k).wait_recv()
                forward_copy(k).start()
        for k, (dr, dc) in enumerate(DIRECTIONS):
            @pl.when(exists(-dr, -dc))
            def _():
                forward_copy(k).wait()

            @pl.when(exists(dr, dc))
            def _():
                halo_copy(k).wait_send()

    start_halo()
    probe_copy.start()
    for part in range(2):
        cosine, sine = table_ref[part], table_ref[2 + part]
        rights[part, :side, :side] = cosine
        rights[part, :side, side:] = -sine
        rights[part, side:, :side] = sine
        rights[part, side:, side:] = cosine
        lefts[part, :side, :side] = cosine
        lefts[part, :side, side:] = sine
        lefts[part, side:, :side] = -sine
        lefts[part, side:, side:] = cosine
    row_at = rows_ref[m] + half
    col_at = cols_ref[m] + half
    live = (m < counts_ref[0]).astype(jnp.float32)
    probe_copy.wait()
    width = 3 * half
    row_back, col_back = lax.rem(width - row_at, width), lax.rem(width - col_at, width)

    def swap_in(x):
        top = jnp.concatenate([x[:side, :side], x[side:, :side]], axis=1)
        return jnp.concatenate([top, jnp.concatenate([x[:side, side:], x[side:, side:]], axis=1)], axis=0)

    def iteration(step, carry):
        finish_halo()
        window = [
            pltpu.roll(pltpu.roll(ext[plane], row_back, axis=0)[:side], col_back, axis=1)[:, :side]
            for plane in range(2)
        ]
        probes = [(probe_ref[0, 0], probe_ref[0, 1]), (probe_other[0], probe_other[1])]
        real = [pr * window[0] - pi * window[1] for pr, pi in probes]
        imag = [pr * window[1] + pi * window[0] for pr, pi in probes]
        exit_wave = jnp.concatenate([jnp.concatenate(real, axis=1), jnp.concatenate(imag, axis=1)], axis=0)
        left, right = (lefts[0], lefts[1]), (rights[0], rights[1])
        middle = swap_in(dot3(left, split(exit_wave)))
        wave = dot3(split(middle), right)
        square = wave * wave
        intensity = square[:side, :side] + square[:side, side:] + square[side:, :side] + square[side:, side:]
        residual = live * (intensity - measured_ref[m].astype(jnp.float32))
        residual = jnp.concatenate([residual, residual], axis=1)
        back = wave * jnp.concatenate([residual, residual], axis=0)
        back = swap_in(dot3(split(back), left))
        back = dot3(right, split(back))
        g = [jnp.zeros((side, side), jnp.float32)] * 2
        for q, (pr, pi) in enumerate(probes):
            br = back[:side, side * q:side * (q + 1)]
            bi = back[side:, side * q:side * (q + 1)]
            g = [g[0] + (pr * br + pi * bi), g[1] + (pr * bi - pi * br)]
        for plane in range(2):
            wide = jnp.concatenate([g[plane], jnp.zeros((side, half), jnp.float32)], axis=1)
            wide = pltpu.roll(wide, col_at, axis=1)
            wide = jnp.concatenate([wide, jnp.zeros((half, width), jnp.float32)], axis=0)
            grad[plane] = pltpu.roll(wide, row_at, axis=0)
        grad_copy.start()
        grad_copy.wait()
        grad[m] = grad[m] + partner_grad[...]
        for k, (dr, dc) in enumerate(DIRECTIONS):
            @pl.when(exists(dr, dc))
            def _():
                fold_copy(k).start()
        for k, (dr, dc) in enumerate(DIRECTIONS):
            @pl.when(exists(-dr, -dc))
            def _():
                fold_copy(k).wait_recv()
        total = grad[m, half:2 * half, half:2 * half]
        for k in range(len(DIRECTIONS)):
            total = total + received[k]
        ext[m, half:2 * half, half:2 * half] = ext[m, half:2 * half, half:2 * half] - STEP * total

        @pl.when(step < ITERS - 1)
        def _():
            start_halo()
        center_copy.start()
        for k, (dr, dc) in enumerate(DIRECTIONS):
            @pl.when(exists(dr, dc))
            def _():
                fold_copy(k).wait_send()
        center_copy.wait()
        return carry

    lax.fori_loop(0, ITERS, iteration, 0)
    out_ref[0] = ext[0, half:2 * half, half:2 * half]
    out_ref[1] = ext[1, half:2 * half, half:2 * half]


def body(object_field, probe_modes, measured, offset_rows, offset_cols, pattern_counts):
    side = probe_modes.shape[-1]
    half = object_field.shape[-1]
    width = 3 * half
    smem = pl.BlockSpec(memory_space=pltpu.SMEM)
    vmem = pl.BlockSpec(memory_space=pltpu.VMEM)
    ways = len(DIRECTIONS)
    dma = pltpu.SemaphoreType.DMA
    return pl.pallas_call(
        kernel,
        out_shape=jax.ShapeDtypeStruct(object_field.shape, jnp.float32),
        in_specs=[smem] * 3 + [vmem] * 4,
        out_specs=vmem,
        scratch_shapes=[
            pltpu.VMEM((2, width, width), jnp.float32),
            pltpu.VMEM((2, width, width), jnp.float32),
            pltpu.VMEM((width, width), jnp.float32),
            pltpu.VMEM((ways, half, half), jnp.float32),
            pltpu.VMEM((2, side, side), jnp.float32),
            pltpu.VMEM((2, 2 * side, 2 * side), jnp.bfloat16),
            pltpu.VMEM((2, 2 * side, 2 * side), jnp.bfloat16),
            dma((ways,)), dma((ways,)), dma((ways,)), dma((ways,)), dma((ways,)), dma((ways,)),
            dma((3,)), dma((3,)),
        ],
        compiler_params=pltpu.CompilerParams(
            collective_id=0, has_side_effects=True, vmem_limit_bytes=56 * 1024 * 1024),
    )(offset_rows[0, 0], offset_cols[0, 0], pattern_counts[0], object_field, probe_modes, measured[0, 0],
      jnp.asarray(dft_tables(side)))


def solution(mesh):
    in_specs = (
        P(None, ("groups", "row"), "col"),
        P("mode", None, None, None),
        P(("groups", "row"), "col", None, None, None),
        P(("groups", "row"), "col", None),
        P(("groups", "row"), "col", None),
        P(("groups", "row"), "col"),
    )
    out_specs = P(None, ("groups", "row"), "col")
    return jax.shard_map(body, mesh=mesh, in_specs=in_specs, out_specs=out_specs, check_vma=False)
```

profile of v0, /device:TPU:9, one launch (start us, length us, event | category | flops | bytes accessed | tf_op | source)
XLA Modules:
  0.0 47.2 jit_solution(5194896815774754837)
XLA Ops:
  0.7 45.0 %shard_map.73 = f32[2,128,128]{2,1,0:T(8,128)} custom-call(s32[2]{0:T(128)} %bitcast.6, s32[2]{0:T(128)} %bitcast.7, s32[1]{0:T(128)} %bitcast.4.counts_ref, f32[2,128,128]{2,1,0:T(8,128)} %field_ref.1, f32[1,2,256,256]{3,2,1,0:T(8,128)} %probe_ref.1, bf16[2,256,256]{2,1,0:T(8,128)(2,1)} %bitcast.5, bf16[4,256,256]{2,1,0:T(8,128)(2,1)} %constant.2.clone.table_ref), custom_call_target="tpu_custom_call" | custom-call | tf_op jit(solution)/shard_map/pallas_call | solution.py:216
  45.7 1.6 %copy.10 = f32[2,128,128]{2,1,0:T(8,128)} copy(f32[2,128,128]{2,1,0:T(8,128)} %shard_map.73) | data formatting | bytes 262144
where the time goes:
time: 47.4 us; the launch traced here: 47.2 us
  Pallas kernels  45 us (95%)
  local copies, waits for them, and re-layouts  1.57 us (3%)
  between operations  0.66 us (1%)
    pallas_call x1, Pallas kernels, body(): pl.pallas_call(kernel, out_shape=jax.ShapeDtypeStruct(object_field.shape,...  45 us
    unnamed x1, local copies, waits for them, and re-layouts  1.57 us

commit v1 on v0

--- a/solution.py
+++ b/solution.py
@@ -15,14 +15,15 @@
 
 
 def dft_tables(side):
-    index = np.arange(side)
-    angles = (index[:, None] * index[None, :] % side) * (2.0 * np.pi / side)
+    index = np.arange(side // 2)
     tables = []
-    for table in (np.cos(angles), np.sin(angles)):
-        table = (table / np.sqrt(side)).astype(np.float32)
-        high = table.astype(jnp.bfloat16)
-        low = (table - high.astype(np.float32)).astype(jnp.bfloat16)
-        tables += [high, low]
+    for parity in range(2):
+        angles = ((2 * index[:, None] + parity) * index[None, :] % side) * (2.0 * np.pi / side)
+        cosine, sine = np.cos(angles) / np.sqrt(side), np.sin(angles) / np.sqrt(side)
+        table = np.block([[cosine, sine], [-sine, cosine]]).astype(np.float32)
+        for form in (table, table.T):
+            high = form.astype(jnp.bfloat16)
+            tables += [high, (form - high.astype(np.float32)).astype(jnp.bfloat16)]
     return np.stack(tables)
 
 
@@ -40,7 +41,7 @@
 
 
 def kernel(rows_ref, cols_ref, counts_ref, field_ref, probe_ref, measured_ref, table_ref, out_ref,
-           ext, grad, partner_grad, received, probe_other, lefts, rights,
+           ext, grad, raw, partner_raw, received, probe_other, target,
            halo_send, halo_recv, fwd_send, fwd_recv, fold_send, fold_recv, own_send, own_recv):
     side = probe_ref.shape[-1]
     half = field_ref.shape[-1]
@@ -96,7 +97,7 @@
                       {"row": r + dr, "col": c + dc})
 
     probe_copy = remote(probe_ref.at[0], probe_other, own_send.at[0], own_recv.at[0], partner)
-    grad_copy = remote(grad.at[other], partner_grad, own_send.at[1], own_recv.at[1], partner)
+    grad_copy = remote(raw.at[other], partner_raw, own_send.at[1], own_recv.at[1], partner)
     center_copy = remote(block(ext, m, 0, 0), block(ext, m, 0, 0), own_send.at[2], own_recv.at[2], partner)
 
     def start_halo():
@@ -122,16 +123,15 @@
 
     start_halo()
     probe_copy.start()
-    for part in range(2):
-        cosine, sine = table_ref[part], table_ref[2 + part]
-        rights[part, :side, :side] = cosine
-        rights[part, :side, side:] = -sine
-        rights[part, side:, :side] = sine
-        rights[part, side:, side:] = cosine
-        lefts[part, :side, :side] = cosine
-        lefts[part, :side, side:] = sine
-        lefts[part, side:, :side] = -sine
-        lefts[part, side:, side:] = cosine
+    lines = lax.broadcasted_iota(jnp.int32, (side, side), 0)
+    lanes = lax.broadcasted_iota(jnp.int32, (side, side), 1)
+
+    def sorted_by_parity(along, across):
+        return (along == jnp.where(across < half, 2 * across, 2 * (across - half) + 1)).astype(
+            jnp.float32).astype(jnp.bfloat16)
+
+    target[...] = dot(dot(sorted_by_parity(lanes, lines), measured_ref[m]).astype(jnp.bfloat16),
+                      sorted_by_parity(lines, lanes))
     row_at = rows_ref[m] + half
     col_at = cols_ref[m] + half
     live = (m < counts_ref[0]).astype(jnp.float32)
@@ -139,9 +139,14 @@
     width = 3 * half
     row_back, col_back = lax.rem(width - row_at, width), lax.rem(width - col_at, width)
 
-    def swap_in(x):
-        top = jnp.concatenate([x[:side, :side], x[side:, :side]], axis=1)
-        return jnp.concatenate([top, jnp.concatenate([x[:side, side:], x[side:, side:]], axis=1)], axis=0)
+    def place(g, row, col):
+        wide = pltpu.roll(jnp.concatenate([g, jnp.zeros((side, half), jnp.float32)], axis=1), col, axis=1)
+        return pltpu.roll(jnp.concatenate([wide, jnp.zeros((half, width), jnp.float32)], axis=0), row, axis=0)
+
+    def halves(x, axis):
+        first = lax.slice_in_dim(x, 0, half, axis=axis)
+        last = lax.slice_in_dim(x, half, side, axis=axis)
+        return first + last, first - last
 
     def iteration(step, carry):
         finish_halo()
@@ -152,30 +157,54 @@
         probes = [(probe_ref[0, 0], probe_ref[0, 1]), (probe_other[0], probe_other[1])]
         real = [pr * window[0] - pi * window[1] for pr, pi in probes]
         imag = [pr * window[1] + pi * window[0] for pr, pi in probes]
-        exit_wave = jnp.concatenate([jnp.concatenate(real, axis=1), jnp.concatenate(imag, axis=1)], axis=0)
-        left, right = (lefts[0], lefts[1]), (rights[0], rights[1])
-        middle = swap_in(dot3(left, split(exit_wave)))
-        wave = dot3(split(middle), right)
-        square = wave * wave
-        intensity = square[:side, :side] + square[:side, side:] + square[side:, :side] + square[side:, side:]
-        residual = live * (intensity - measured_ref[m].astype(jnp.float32))
-        residual = jnp.concatenate([residual, residual], axis=1)
-        back = wave * jnp.concatenate([residual, residual], axis=0)
-        back = swap_in(dot3(split(back), left))
-        back = dot3(right, split(back))
+        real, imag = jnp.concatenate(real, axis=1), jnp.concatenate(imag, axis=1)
+        table = [[(table_ref[4 * p + 2 * t], table_ref[4 * p + 2 * t + 1]) for t in range(2)] for p in range(2)]
+        real, imag = halves(real, 0), halves(imag, 0)
+        middle = [
+            dot3(table[p][0], split(jnp.concatenate([real[p], imag[p]], axis=0))) for p in range(2)
+        ]
+        stacked = [[], []]
+        for p in range(2):
+            for q in range(2):
+                part = middle[p][:, side * q:side * (q + 1)]
+                mixed = halves(part, 1)
+                for t in range(2):
+                    stacked[t].append(jnp.concatenate([mixed[t][:half], mixed[t][half:]], axis=1))
+        wave = [dot3(split(jnp.concatenate(stacked[t], axis=0)), table[t][1]) for t in range(2)]
+        back = []
+        for t in range(2):
+            square = wave[t] * wave[t]
+            square = square[:, :half] + square[:, half:]
+            parts = []
+            for p in range(2):
+                intensity = square[side * p:side * p + half] + square[side * p + half:side * (p + 1)]
+                residual = live * (intensity - target[half * p:half * (p + 1), half * t:half * (t + 1)])
+                residual = jnp.concatenate([residual, residual], axis=1)
+                parts += [residual, residual]
+            back.append(dot3(split(wave[t] * jnp.concatenate(parts, axis=0)), table[t][0]))
+        both = (back[0] + back[1], back[0] - back[1])
+        last = []
+        for p in range(2):
+            sides = []
+            for plane in range(2):
+                sides.append(jnp.concatenate(
+                    [both[t][side * p + half * q:side * p + half * (q + 1), half * plane:half * (plane + 1)]
+                     for q in range(2) for t in range(2)], axis=1))
+            last.append(dot3(table[p][1], split(jnp.concatenate(sides, axis=0))))
+        both = (last[0] + last[1], last[0] - last[1])
         g = [jnp.zeros((side, side), jnp.float32)] * 2
         for q, (pr, pi) in enumerate(probes):
-            br = back[:side, side * q:side * (q + 1)]
-            bi = back[side:, side * q:side * (q + 1)]
+            br, bi = [
+                jnp.concatenate([part[half * plane:half * (plane + 1), side * q:side * (q + 1)] for part in both], axis=0)
+                for plane in range(2)
+            ]
             g = [g[0] + (pr * br + pi * bi), g[1] + (pr * bi - pi * br)]
-        for plane in range(2):
-            wide = jnp.concatenate([g[plane], jnp.zeros((side, half), jnp.float32)], axis=1)
-            wide = pltpu.roll(wide, col_at, axis=1)
-            wide = jnp.concatenate([wide, jnp.zeros((half, width), jnp.float32)], axis=0)
-            grad[plane] = pltpu.roll(wide, row_at, axis=0)
+        raw[0] = g[0]
+        raw[1] = g[1]
         grad_copy.start()
+        own = place(raw[m], row_at, col_at)
         grad_copy.wait()
-        grad[m] = grad[m] + partner_grad[...]
+        grad[m] = own + place(partner_raw[...], rows_ref[other] + half, cols_ref[other] + half)
         for k, (dr, dc) in enumerate(DIRECTIONS):
             @pl.when(exists(dr, dc))
             def _():
@@ -221,11 +250,11 @@
         scratch_shapes=[
             pltpu.VMEM((2, width, width), jnp.float32),
             pltpu.VMEM((2, width, width), jnp.float32),
-            pltpu.VMEM((width, width), jnp.float32),
+            pltpu.VMEM((2, side, side), jnp.float32),
+            pltpu.VMEM((side, side), jnp.float32),
             pltpu.VMEM((ways, half, half), jnp.float32),
             pltpu.VMEM((2, side, side), jnp.float32),
-            pltpu.VMEM((2, 2 * side, 2 * side), jnp.bfloat16),
-            pltpu.VMEM((2, 2 * side, 2 * side), jnp.bfloat16),
+            pltpu.VMEM((side, side), jnp.float32),
             dma((ways,)), dma((ways,)), dma((ways,)), dma((ways,)), dma((ways,)), dma((ways,)),
             dma((3,)), dma((3,)),
         ],

time: 47.4 us -> 43.7 us (0.922)
  Pallas kernels: 45 us -> 41.3 us
    pallas_call x1, Pallas kernels: 45 us -> 41.3 us  [body(): pl.pallas_call(kernel, out_shape=jax.ShapeDtypeStruct(object_field.shape,...]
where the time goes in v1:
time: 43.7 us; the launch traced here: 43.5 us
  Pallas kernels  41.3 us (95%)
  local copies, waits for them, and re-layouts  1.57 us (4%)
  between operations  0.66 us (2%)
    pallas_call x1, Pallas kernels, body(): pl.pallas_call(kernel, out_shape=jax.ShapeDtypeStruct(object_field.shape,...  41.3 us
    unnamed x1, local copies, waits for them, and re-layouts  1.57 us

profile of v1, /device:TPU:9, one launch (start us, length us, event | category | flops | bytes accessed | tf_op | source)
XLA Modules:
  0.0 43.5 jit_solution(4907249284200083330)
XLA Ops:
  0.7 41.3 %shard_map.73 = f32[2,128,128]{2,1,0:T(8,128)} custom-call(s32[2]{0:T(128)} %bitcast.6, s32[2]{0:T(128)} %bitcast.7, s32[1]{0:T(128)} %bitcast.4.counts_ref, f32[2,128,128]{2,1,0:T(8,128)} %field_ref.1, f32[1,2,256,256]{3,2,1,0:T(8,128)} %probe_ref.1, bf16[2,256,256]{2,1,0:T(8,128)(2,1)} %bitcast.5, bf16[8,256,256]{2,1,0:T(8,128)(2,1)} %constant.2.clone.table_ref), custom_call_target="tpu_custom_call" | custom-call | tf_op jit(solution)/shard_map/pallas_call | solution.py:245
  42.0 1.6 %copy.10 = f32[2,128,128]{2,1,0:T(8,128)} copy(f32[2,128,128]{2,1,0:T(8,128)} %shard_map.73) | data formatting | bytes 262144
